TPU v7x, 512 devices: a whole 4x8x8 slice. The times are simulated.
512 devices in a mesh: blk: 64 (over z_hi, y, core), rep: 8 (over z_lo, x).
Axes of the slice: x: 4, y: 8, z: 8 (z_hi: 4, z_lo: 2; z = z_hi * 2 + z_lo), core: 2. Of those that a mesh axis runs over, the one named last changes fastest.
Arguments:
- features: bfloat16 [32768, 128], P('blk'), may hold values from -6 to 6
- weight: bfloat16 [128, 256], replicated, may hold values from -0.5 to 0.5
- tile_vals: bfloat16 [64, 8, 8, 12, 128, 128], P('blk', 'rep'), may hold values from -0.0390625 to 0.0390625
- tile_pos: int32 [64, 8, 8, 12], P('blk', 'rep'), may hold values from 0 to 15, as said below
- tile_count: int32 [64, 8, 8], P('blk', 'rep'), may hold values from 1 to 12, as said below
- cotangent: bfloat16 [32768, 256], P(('blk', 'rep')), may hold values from -6 to 6
Outputs:
- activations: bfloat16 [32768, 256], P(('blk', 'rep'))
- feat_grad: bfloat16 [32768, 128], P(('blk', 'rep'))
- weight_grad: float32 [128, 256], replicated
Inputs may be any that keep to these rules, and one draw needn't show every extreme that they name: `tile_pos`: within one row group, copy and section the entries are distinct. `tile_count`: row group 0 has all 12 slots live in every copy and section.
All inputs are finite; a program needn't handle non-finite values.
Results may differ from a plain program's by a relative error of at most 0.014.
Values may be sent and summed in bfloat16 or wider, within the bound.
A program may use at most 128 MiB of HBM per device.

v0:
```python
import jax
import jax.numpy as jnp
from jax import lax
from jax.sharding import PartitionSpec as P


def passed_along(block, axis, distance):
    devices = range(lax.axis_size(axis))
    route = [((i - distance) % len(devices), i) for i in devices]
    return lax.ppermute(block, axis, route)


def gelu_tanh(value):
    return jax.nn.gelu(value, approximate=True)


def section_forward(tile_block, positions, live_count, current, blocks):
    tile_size = tile_block.shape[-1]
    columns = current.reshape(blocks, tile_size, current.shape[-1])
    picked = columns[positions % blocks]
    live_mask = (jnp.arange(tile_block.shape[0], dtype=jnp.int32) < live_count).astype(jnp.float32)
    product = jnp.einsum("tik,tkf->tif", tile_block, picked, preferred_element_type=jnp.float32)
    product = product * live_mask[:, None, None]
    placing = (
        (positions // blocks)[:, None] == jnp.arange(blocks, dtype=jnp.int32)[None, :]
    ).astype(jnp.float32)
    return jnp.einsum("tn,tif->nif", placing, product).reshape(
        blocks * tile_size, current.shape[-1]
    )


def section_backward(tile_block, positions, live_count, grad_rows, blocks):
    tile_size = tile_block.shape[-1]
    rows_view = grad_rows.reshape(blocks, tile_size, grad_rows.shape[-1])
    picked = rows_view[positions // blocks]
    live_mask = (jnp.arange(tile_block.shape[0], dtype=jnp.int32) < live_count).astype(jnp.float32)
    product = jnp.einsum("tki,tkf->tif", tile_block, picked, preferred_element_type=jnp.float32)
    product = product * live_mask[:, None, None]
    placing = (
        (positions % blocks)[:, None] == jnp.arange(blocks, dtype=jnp.int32)[None, :]
    ).astype(jnp.float32)
    return jnp.einsum("tn,tif->nif", placing, product).reshape(
        blocks * tile_size, grad_rows.shape[-1]
    )


def skew_forward(value, rep_index, rep_size):
    for bit_index in range((rep_size - 1).bit_length()):
        moved = passed_along(value, "blk", 1 << bit_index)
        value = jnp.where(jnp.right_shift(rep_index, bit_index) % 2 == 1, moved, value)
    return value


def skew_back(value, rep_index, rep_size):
    for bit_index in range((rep_size - 1).bit_length()):
        moved = passed_along(value, "blk", -(1 << bit_index))
        value = jnp.where(jnp.right_shift(rep_index, bit_index) % 2 == 1, moved, value)
    return value


def local(features, weight, tile_vals, tile_pos, tile_count, cotangent):
    rep_size = lax.axis_size("rep")
    rep_index = lax.axis_index("rep")
    local_tiles = tile_vals[0, 0]
    local_pos = tile_pos[0, 0]
    local_count = tile_count[0, 0]
    section_count = local_tiles.shape[0]
    tile_size = local_tiles.shape[-1]
    blocks = features.shape[0] // tile_size
    rows_share = features.shape[0] // rep_size
    row_start = rep_index * rows_share

    def section_terms(section, current):
        return section_forward(
            lax.dynamic_index_in_dim(local_tiles, section, 0, keepdims=False),
            lax.dynamic_index_in_dim(local_pos, section, 0, keepdims=False),
            lax.dynamic_index_in_dim(local_count, section, 0, keepdims=False),
            current,
            blocks,
        )

    hidden = jnp.dot(features, weight, preferred_element_type=jnp.float32).astype(jnp.bfloat16)
    seeded = skew_forward(hidden, rep_index, rep_size)
    zeros_total = jnp.zeros((features.shape[0], weight.shape[1]), jnp.float32)

    def one_step(section, state):
        current, total = state
        total = total + section_terms(section, current)
        current = passed_along(current, "blk", rep_size)
        return (current, total)

    current, total = lax.fori_loop(0, section_count - 1, one_step, (seeded, zeros_total))
    total = total + section_terms(section_count - 1, current)
    pre = lax.psum_scatter(total, "rep", scatter_dimension=0, tiled=True)
    outputs, pullback = jax.vjp(gelu_tanh, pre)
    activations = outputs.astype(jnp.bfloat16)
    pre_grad = pullback(cotangent.astype(jnp.float32))[0].astype(jnp.bfloat16)
    grad_rows = lax.all_gather(pre_grad, "rep", axis=0, tiled=True)

    def back_terms(section):
        return section_backward(
            lax.dynamic_index_in_dim(local_tiles, section, 0, keepdims=False),
            lax.dynamic_index_in_dim(local_pos, section, 0, keepdims=False),
            lax.dynamic_index_in_dim(local_count, section, 0, keepdims=False),
            grad_rows,
            blocks,
        )

    def back_step(section, carried):
        return passed_along(carried + back_terms(section), "blk", rep_size)

    carried = lax.fori_loop(0, section_count, back_step, zeros_total)
    carried = skew_back(carried, rep_index, rep_size)
    hidden_grad = lax.psum_scatter(carried, "rep", scatter_dimension=0, tiled=True).astype(
        jnp.bfloat16
    )
    feat_grad = lax.dot_general(
        hidden_grad, weight, (((1,), (1,)), ((), ())), preferred_element_type=jnp.float32
    ).astype(jnp.bfloat16)
    feat_rows = lax.dynamic_slice_in_dim(features, row_start, rows_share, 0)
    partial_grad = lax.dot_general(
        feat_rows, hidden_grad, (((0,), (0,)), ((), ())), preferred_element_type=jnp.float32
    )
    weight_grad = lax.psum(partial_grad, ("blk", "rep"))
    return (activations, feat_grad, weight_grad)


def solution(mesh):
    placed = (
        P("blk", None),
        P(),
        P("blk", "rep", None, None, None, None),
        P("blk", "rep", None, None),
        P("blk", "rep", None),
        P(("blk", "rep"), None),
    )
    return jax.shard_map(
        local,
        mesh=mesh,
        in_specs=placed,
        out_specs=(P(("blk", "rep"), None), P(("blk", "rep"), None), P()),
        check_vma=False,
    )
```

profile of v0, /device:TPU:1, one launch (start us, length us, event | category | flops | bytes accessed | tf_op | source)
XLA Modules:
  0.0 1005.6 jit_solution(1865556596306336657)
XLA Ops:
  9.1 4.6 collective-permute-start.2
  15.0 3.9 collective-permute-done.2
  18.9 1.9 collective-permute-start.3
  21.6 14.1 %collective-permute-done.3 = bf16[512,256]{1,0:T(8,128)(2,1)S(1)} collective-permute-done((bf16[512,256]{1,0:T(8,128)(2,1)S(1)}, bf16[512,256]{1,0:T(8,128)(2,1)S(1)}, u32[]{:S(2)}, u32[]{:S(2)}) %collective-permute-start.3) | collective-permute-done | bytes 262176 | tf_op jit(solution)/shard_map/ppermute | solution.py:10
  35.7 1.9 collective-permute-start.4
  38.4 12.9 %collective-permute-done.4 = bf16[512,256]{1,0:T(8,128)(2,1)S(1)} collective-permute-done((bf16[512,256]{1,0:T(8,128)(2,1)S(1)}, bf16[512,256]{1,0:T(8,128)(2,1)S(1)}, u32[]{:S(2)}, u32[]{:S(2)}) %collective-permute-start.4) | collective-permute-done | bytes 262176 | tf_op jit(solution)/shard_map/ppermute | solution.py:10
  51.4 140.1 %while.34 = (s32[]{:T(128)}, bf16[512,256]{1,0:T(8,128)(2,1)S(1)}, f32[512,256]{1,0:T(8,128)S(1)}, s32[8,12]{1,0:T(8,128)S(1)}, bf16[8,12,128,128]{3,2,1,0:T(8,1...) while((s32[]{:T(128)}, bf16[512,256]{1,0:T(8,128)(2,1)S(1)}, f32[512,256]{1,0:T(8,128)S(1)}, ...), condition=%wide.region_1.2_spmd.clone, body=%wide.region_0.1_spmd.clone.sunk | while | flops 104465824 | bytes 10621531 | solution.py:92
  51.4 1.9 collective-permute-start.1
  57.8 10.0 collective-permute-done.1
  67.8 1.9 collective-permute-start.1
  74.2 13.7 %collective-permute-done.1 = bf16[512,256]{1,0:T(8,128)(2,1)S(1)} collective-permute-done((bf16[512,256]{1,0:T(8,128)(2,1)S(1)}, bf16[512,256]{1,0:T(8,128)(2,1)S(1)}, u32[]{:S(2)}, u32[]{:S(2)}) %collective-permute-start.1) | collective-permute-done | bytes 262176 | tf_op jit(solution)/shard_map/while/body/eval_jaxpr/ppermute | solution.py:10
  87.9 1.9 collective-permute-start.1
  94.3 14.5 %collective-permute-done.1 = bf16[512,256]{1,0:T(8,128)(2,1)S(1)} collective-permute-done((bf16[512,256]{1,0:T(8,128)(2,1)S(1)}, bf16[512,256]{1,0:T(8,128)(2,1)S(1)}, u32[]{:S(2)}, u32[]{:S(2)}) %collective-permute-start.1) | collective-permute-done | bytes 262176 | tf_op jit(solution)/shard_map/while/body/eval_jaxpr/ppermute | solution.py:10
  108.8 1.9 collective-permute-start.1
  115.2 14.4 %collective-permute-done.1 = bf16[512,256]{1,0:T(8,128)(2,1)S(1)} collective-permute-done((bf16[512,256]{1,0:T(8,128)(2,1)S(1)}, bf16[512,256]{1,0:T(8,128)(2,1)S(1)}, u32[]{:S(2)}, u32[]{:S(2)}) %collective-permute-start.1) | collective-permute-done | bytes 262176 | tf_op jit(solution)/shard_map/while/body/eval_jaxpr/ppermute | solution.py:10
  129.6 1.9 collective-permute-start.1
  136.0 14.3 %collective-permute-done.1 = bf16[512,256]{1,0:T(8,128)(2,1)S(1)} collective-permute-done((bf16[512,256]{1,0:T(8,128)(2,1)S(1)}, bf16[512,256]{1,0:T(8,128)(2,1)S(1)}, u32[]{:S(2)}, u32[]{:S(2)}) %collective-permute-start.1) | collective-permute-done | bytes 262176 | tf_op jit(solution)/shard_map/while/body/eval_jaxpr/ppermute | solution.py:10
  150.3 2.6 collective-permute-start.1
  157.4 12.5 %collective-permute-done.1 = bf16[512,256]{1,0:T(8,128)(2,1)S(1)} collective-permute-done((bf16[512,256]{1,0:T(8,128)(2,1)S(1)}, bf16[512,256]{1,0:T(8,128)(2,1)S(1)}, u32[]{:S(2)}, u32[]{:S(2)}) %collective-permute-start.1) | collective-permute-done | bytes 262176 | tf_op jit(solution)/shard_map/while/body/eval_jaxpr/ppermute | solution.py:10
  169.9 3.7 collective-permute-start.1
  178.1 13.4 %collective-permute-done.1 = bf16[512,256]{1,0:T(8,128)(2,1)S(1)} collective-permute-done((bf16[512,256]{1,0:T(8,128)(2,1)S(1)}, bf16[512,256]{1,0:T(8,128)(2,1)S(1)}, u32[]{:S(2)}, u32[]{:S(2)}) %collective-permute-start.1) | collective-permute-done | bytes 262176 | tf_op jit(solution)/shard_map/while/body/eval_jaxpr/ppermute | solution.py:10
  192.1 2.6 fusion.26
  194.7 2.2 copy.14
  198.3 52.4 %reduce-scatter.3.cloned.1.call-done = f32[64,256]{1,0:T(8,128)} async-done(((f32[512,256]{1,0:T(8,128)}), f32[64,256]{1,0:T(8,128)}) %reduce-scatter.3.cloned.1.call-update) | async-done | bytes 65552 | tf_op jit(solution)/shard_map/reduce_scatter | solution.py:94
  252.2 22.0 %all_gather.3 = bf16[512,256]{1,0:T(8,128)(2,1)S(1)} all-gather(bf16[64,256]{1,0:T(8,128)(2,1)S(1)} %get-tuple-element.366), channel_id=1, replica_groups=mesh['blk'=64,'rep'=8] {'rep'}, dimensions={0}, use_global_device_ids=true | all-gather | bytes 294912 | tf_op jit(solution)/shard_map/all_gather | solution.py:98
  274.2 247.6 %while.33 = (s32[]{:T(128)}, f32[512,256]{1,0:T(8,128)S(1)}, s32[8,12]{1,0:T(8,128)S(1)}, bf16[8,12,128,128]{3,2,1,0:T(8,128)(2,1)}, bf16[512,256]{1,0:T(8,128)(2,1)S(1)}, /*index=5*/s32[8]{0:T(128)S(1)}, s32[]{:T(128)}) while((s32[]{:T(128)}, f32[512,256]{1,0:T(8,128)S(1)}, s32[8,12]{1,0:T(8,128)S(1)}, bf16[8,12,128,128]{3,2,1,0:T(8,128)(2,1)}, ...), condition=%wide.region_4.5_spmd, body=%wide.region_3.4_spmd.sunk | while | flops 104334752 | bytes 11146301 | solution.py:112
  278.7 6.7 collective-permute-start
  285.5 15.3 %collective-permute-done = f32[512,256]{1,0:T(8,128)S(1)} collective-permute-done((f32[512,256]{1,0:T(8,128)S(1)}, f32[512,256]{1,0:T(8,128)S(1)}, u32[]{:S(2)}, u32[]{:S(2)}) %collective-permute-start) | collective-permute-done | bytes 524320 | tf_op jit(solution)/shard_map/while/body/eval_jaxpr/ppermute | solution.py:10
  305.3 1.9 collective-permute-start
  307.2 23.0 %collective-permute-done = f32[512,256]{1,0:T(8,128)S(1)} collective-permute-done((f32[512,256]{1,0:T(8,128)S(1)}, f32[512,256]{1,0:T(8,128)S(1)}, u32[]{:S(2)}, u32[]{:S(2)}) %collective-permute-start) | collective-permute-done | bytes 524320 | tf_op jit(solution)/shard_map/while/body/eval_jaxpr/ppermute | solution.py:10
  334.7 1.9 collective-permute-start
  336.7 28.7 %collective-permute-done = f32[512,256]{1,0:T(8,128)S(1)} collective-permute-done((f32[512,256]{1,0:T(8,128)S(1)}, f32[512,256]{1,0:T(8,128)S(1)}, u32[]{:S(2)}, u32[]{:S(2)}) %collective-permute-start) | collective-permute-done | bytes 524320 | tf_op jit(solution)/shard_map/while/body/eval_jaxpr/ppermute | solution.py:10
  369.8 1.9 collective-permute-start
  371.8 27.3 %collective-permute-done = f32[512,256]{1,0:T(8,128)S(1)} collective-permute-done((f32[512,256]{1,0:T(8,128)S(1)}, f32[512,256]{1,0:T(8,128)S(1)}, u32[]{:S(2)}, u32[]{:S(2)}) %collective-permute-start) | collective-permute-done | bytes 524320 | tf_op jit(solution)/shard_map/while/body/eval_jaxpr/ppermute | solution.py:10
  403.5 1.9 collective-permute-start
  405.4 26.0 %collective-permute-done = f32[512,256]{1,0:T(8,128)S(1)} collective-permute-done((f32[512,256]{1,0:T(8,128)S(1)}, f32[512,256]{1,0:T(8,128)S(1)}, u32[]{:S(2)}, u32[]{:S(2)}) %collective-permute-start) | collective-permute-done | bytes 524320 | tf_op jit(solution)/shard_map/while/body/eval_jaxpr/ppermute | solution.py:10
  435.9 1.9 collective-permute-start
  437.8 26.0 %collective-permute-done = f32[512,256]{1,0:T(8,128)S(1)} collective-permute-done((f32[512,256]{1,0:T(8,128)S(1)}, f32[512,256]{1,0:T(8,128)S(1)}, u32[]{:S(2)}, u32[]{:S(2)}) %collective-permute-start) | collective-permute-done | bytes 524320 | tf_op jit(solution)/shard_map/while/body/eval_jaxpr/ppermute | solution.py:10
  468.3 1.9 collective-permute-start
  470.2 20.2 %collective-permute-done = f32[512,256]{1,0:T(8,128)S(1)} collective-permute-done((f32[512,256]{1,0:T(8,128)S(1)}, f32[512,256]{1,0:T(8,128)S(1)}, u32[]{:S(2)}, u32[]{:S(2)}) %collective-permute-start) | collective-permute-done | bytes 524320 | tf_op jit(solution)/shard_map/while/body/eval_jaxpr/ppermute | solution.py:10
  496.8 25.0 %collective-permute-done = f32[512,256]{1,0:T(8,128)S(1)} collective-permute-done((f32[512,256]{1,0:T(8,128)S(1)}, f32[512,256]{1,0:T(8,128)S(1)}, u32[]{:S(2)}, u32[]{:S(2)}) %collective-permute-start) | collective-permute-done | bytes 524320 | tf_op jit(solution)/shard_map/while/body/eval_jaxpr/ppermute | solution.py:10
  521.8 27.2 %collective-permute-start.5 = (f32[512,256]{1,0:T(8,128)S(1)}, f32[512,256]{1,0:T(8,128)S(1)}, u32[]{:S(2)}, u32[]{:S(2)}) collective-permute-start(f32[512,256]{1,0:T(8,128)S(1)} %get-tuple-element.320), channel_id=1, source_target_pairs={{8,0},{16,8},{24,16},{32,24},{40,32},{48,40},{56,48},{64,56},{72,6... | collective-permute-start | bytes 1572872 | tf_op jit(solution)/shard_map/ppermute | solution.py:10
  550.6 17.8 %collective-permute-start.6 = (f32[512,256]{1,0:T(8,128)S(1)}, f32[512,256]{1,0:T(8,128)S(1)}, u32[]{:S(2)}, u32[]{:S(2)}) collective-permute-start(f32[512,256]{1,0:T(8,128)S(1)} %broadcast_select_fusion), channel_id=1, source_target_pairs={{16,0},{24,8},{32,16},{40,24},{48,32},{56,40},{64,48},{72,56},{80,... | collective-permute-start | bytes 1572872 | tf_op jit(solution)/shard_map/ppermute | solution.py:10
  568.4 70.9 %collective-permute-done.6 = f32[512,256]{1,0:T(8,128)S(1)} collective-permute-done((f32[512,256]{1,0:T(8,128)S(1)}, f32[512,256]{1,0:T(8,128)S(1)}, u32[]{:S(2)}, u32[]{:S(2)}) %collective-permute-start.6) | collective-permute-done | bytes 524320 | tf_op jit(solution)/shard_map/ppermute | solution.py:10
  639.3 3.4 collective-permute-start.7
  642.8 19.5 %collective-permute-done.7 = f32[512,256]{1,0:T(8,128)S(1)} collective-permute-done((f32[512,256]{1,0:T(8,128)S(1)}, f32[512,256]{1,0:T(8,128)S(1)}, u32[]{:S(2)}, u32[]{:S(2)}) %collective-permute-start.7) | collective-permute-done | bytes 524320 | tf_op jit(solution)/shard_map/ppermute | solution.py:10
  663.2 59.4 %reduce-scatter.5.cloned.1.call-done = f32[64,256]{1,0:T(8,128)} async-done(((f32[512,256]{1,0:T(8,128)}), f32[64,256]{1,0:T(8,128)}) %reduce-scatter.5.cloned.1.call-update) | async-done | bytes 65552 | tf_op jit(solution)/shard_map/reduce_scatter | solution.py:114
  726.0 271.6 %all-reduce.2.cloned.1.call-done = f32[128,256]{1,0:T(8,128)} async-done(((f32[128,256]{1,0:T(8,128)}), f32[128,256]{1,0:T(8,128)}) %all-reduce.2.cloned.1.call-update) | async-done | bytes 131088 | tf_op jit(solution)/shard_map/psum | solution.py:124
  (197 shorter events, 83.9 us)
Async XLA Ops:
  7.2 0.9 copy-start
  7.2 44.2 %copy-start.4 = (s32[1,1,8]{2,1,0:T(1,128)S(1)}, s32[1,1,8]{2,1,0:T(1,128)}, u32[]{:S(2)}) copy-start(s32[1,1,8]{2,1,0:T(1,128)} %param.14) | copy-start | bytes 100
  7.2 31.2 %copy-start.3 = (s32[1,1,8,12]{3,2,1,0:T(8,128)S(1)}, s32[1,1,8,12]{3,2,1,0:T(8,128)}, u32[]{:S(2)}) copy-start(s32[1,1,8,12]{3,2,1,0:T(8,128)} %param.13) | copy-start | bytes 1156
  7.2 243.5 %reduce-scatter.3.cloned.1.call-start = ((), (), s32[]{:S(2)}) async-start(), calls=%async_computation.2 | async-start | bytes 589824 | tf_op jit(solution)/shard_map/reduce_scatter | solution.py:94
  9.1 9.8 collective-permute-start.2
  18.9 16.8 %collective-permute-start.3 = (bf16[512,256]{1,0:T(8,128)(2,1)S(1)}, bf16[512,256]{1,0:T(8,128)(2,1)S(1)}, u32[]{:S(2)}, u32[]{:S(2)}) collective-permute-start(bf16[512,256]{1,0:T(8,128)(2,1)S(1)} %broadcast_select_fusion.1), channel_id=1, source_target_pairs={{496,0},{504,8},{0,16},{8,24},{16,32},{24,40},{32,48},{40,56},{48,... | collective-permute-start | bytes 786440 | tf_op jit(solution)/shard_map/ppermute | solution.py:10
  35.7 15.6 %collective-permute-start.4 = (bf16[512,256]{1,0:T(8,128)(2,1)S(1)}, bf16[512,256]{1,0:T(8,128)(2,1)S(1)}, u32[]{:S(2)}, u32[]{:S(2)}) collective-permute-start(bf16[512,256]{1,0:T(8,128)(2,1)S(1)} %broadcast_select_fusion.3), channel_id=1, source_target_pairs={{480,0},{488,8},{496,16},{504,24},{0,32},{8,40},{16,48},{24,56},{3... | collective-permute-start | bytes 786440 | tf_op jit(solution)/shard_map/ppermute | solution.py:10
  51.4 16.4 %collective-permute-start.1 = (bf16[512,256]{1,0:T(8,128)(2,1)S(1)}, bf16[512,256]{1,0:T(8,128)(2,1)S(1)}, u32[]{:S(2)}, u32[]{:S(2)}) collective-permute-start(bf16[512,256]{1,0:T(8,128)(2,1)S(1)} %copy.31), channel_id=1, source_target_pairs={{448,0},{456,8},{464,16},{472,24},{480,32},{488,40},{496,48},{504,... | collective-permute-start | bytes 786440 | tf_op jit(solution)/shard_map/while/body/eval_jaxpr/ppermute | solution.py:10
  67.8 20.1 %collective-permute-start.1 = (bf16[512,256]{1,0:T(8,128)(2,1)S(1)}, bf16[512,256]{1,0:T(8,128)(2,1)S(1)}, u32[]{:S(2)}, u32[]{:S(2)}) collective-permute-start(bf16[512,256]{1,0:T(8,128)(2,1)S(1)} %copy.31), channel_id=1, source_target_pairs={{448,0},{456,8},{464,16},{472,24},{480,32},{488,40},{496,48},{504,... | collective-permute-start | bytes 786440 | tf_op jit(solution)/shard_map/while/body/eval_jaxpr/ppermute | solution.py:10
  87.9 20.9 %collective-permute-start.1 = (bf16[512,256]{1,0:T(8,128)(2,1)S(1)}, bf16[512,256]{1,0:T(8,128)(2,1)S(1)}, u32[]{:S(2)}, u32[]{:S(2)}) collective-permute-start(bf16[512,256]{1,0:T(8,128)(2,1)S(1)} %copy.31), channel_id=1, source_target_pairs={{448,0},{456,8},{464,16},{472,24},{480,32},{488,40},{496,48},{504,... | collective-permute-start | bytes 786440 | tf_op jit(solution)/shard_map/while/body/eval_jaxpr/ppermute | solution.py:10
  108.8 20.8 %collective-permute-start.1 = (bf16[512,256]{1,0:T(8,128)(2,1)S(1)}, bf16[512,256]{1,0:T(8,128)(2,1)S(1)}, u32[]{:S(2)}, u32[]{:S(2)}) collective-permute-start(bf16[512,256]{1,0:T(8,128)(2,1)S(1)} %copy.31), channel_id=1, source_target_pairs={{448,0},{456,8},{464,16},{472,24},{480,32},{488,40},{496,48},{504,... | collective-permute-start | bytes 786440 | tf_op jit(solution)/shard_map/while/body/eval_jaxpr/ppermute | solution.py:10
  129.6 20.7 %collective-permute-start.1 = (bf16[512,256]{1,0:T(8,128)(2,1)S(1)}, bf16[512,256]{1,0:T(8,128)(2,1)S(1)}, u32[]{:S(2)}, u32[]{:S(2)}) collective-permute-start(bf16[512,256]{1,0:T(8,128)(2,1)S(1)} %copy.31), channel_id=1, source_target_pairs={{448,0},{456,8},{464,16},{472,24},{480,32},{488,40},{496,48},{504,... | collective-permute-start | bytes 786440 | tf_op jit(solution)/shard_map/while/body/eval_jaxpr/ppermute | solution.py:10
  150.3 19.5 %collective-permute-start.1 = (bf16[512,256]{1,0:T(8,128)(2,1)S(1)}, bf16[512,256]{1,0:T(8,128)(2,1)S(1)}, u32[]{:S(2)}, u32[]{:S(2)}) collective-permute-start(bf16[512,256]{1,0:T(8,128)(2,1)S(1)} %copy.31), channel_id=1, source_target_pairs={{448,0},{456,8},{464,16},{472,24},{480,32},{488,40},{496,48},{504,... | collective-permute-start | bytes 786440 | tf_op jit(solution)/shard_map/while/body/eval_jaxpr/ppermute | solution.py:10
  169.9 21.6 %collective-permute-start.1 = (bf16[512,256]{1,0:T(8,128)(2,1)S(1)}, bf16[512,256]{1,0:T(8,128)(2,1)S(1)}, u32[]{:S(2)}, u32[]{:S(2)}) collective-permute-start(bf16[512,256]{1,0:T(8,128)(2,1)S(1)} %copy.31), channel_id=1, source_target_pairs={{448,0},{456,8},{464,16},{472,24},{480,32},{488,40},{496,48},{504,... | collective-permute-start | bytes 786440 | tf_op jit(solution)/shard_map/while/body/eval_jaxpr/ppermute | solution.py:10
  197.2 53.4 %copy-start.2 = (bf16[64,256]{1,0:T(8,128)(2,1)S(1)}, bf16[64,256]{1,0:T(8,128)(2,1)}, u32[]{:S(2)}) copy-start(bf16[64,256]{1,0:T(8,128)(2,1)} %param.15) | copy-start | bytes 98308
  198.3 524.4 %reduce-scatter.5.cloned.1.call-start = ((), (), s32[]{:S(2)}) async-start(), calls=%async_computation.3 | async-start | bytes 589824 | tf_op jit(solution)/shard_map/reduce_scatter | solution.py:114
  278.7 22.1 %collective-permute-start = (f32[512,256]{1,0:T(8,128)S(1)}, f32[512,256]{1,0:T(8,128)S(1)}, u32[]{:S(2)}, u32[]{:S(2)}) collective-permute-start(f32[512,256]{1,0:T(8,128)S(1)} %bitcast_add_fusion.5), channel_id=1, source_target_pairs={{448,0},{456,8},{464,16},{472,24},{480,32},{488,40},{496,48},{504,... | collective-permute-start | bytes 1572872 | tf_op jit(solution)/shard_map/while/body/eval_jaxpr/ppermute | solution.py:10
  305.3 25.0 %collective-permute-start = (f32[512,256]{1,0:T(8,128)S(1)}, f32[512,256]{1,0:T(8,128)S(1)}, u32[]{:S(2)}, u32[]{:S(2)}) collective-permute-start(f32[512,256]{1,0:T(8,128)S(1)} %bitcast_add_fusion.5), channel_id=1, source_target_pairs={{448,0},{456,8},{464,16},{472,24},{480,32},{488,40},{496,48},{504,... | collective-permute-start | bytes 1572872 | tf_op jit(solution)/shard_map/while/body/eval_jaxpr/ppermute | solution.py:10
  334.7 30.6 %collective-permute-start = (f32[512,256]{1,0:T(8,128)S(1)}, f32[512,256]{1,0:T(8,128)S(1)}, u32[]{:S(2)}, u32[]{:S(2)}) collective-permute-start(f32[512,256]{1,0:T(8,128)S(1)} %bitcast_add_fusion.5), channel_id=1, source_target_pairs={{448,0},{456,8},{464,16},{472,24},{480,32},{488,40},{496,48},{504,... | collective-permute-start | bytes 1572872 | tf_op jit(solution)/shard_map/while/body/eval_jaxpr/ppermute | solution.py:10
  369.8 29.2 %collective-permute-start = (f32[512,256]{1,0:T(8,128)S(1)}, f32[512,256]{1,0:T(8,128)S(1)}, u32[]{:S(2)}, u32[]{:S(2)}) collective-permute-start(f32[512,256]{1,0:T(8,128)S(1)} %bitcast_add_fusion.5), channel_id=1, source_target_pairs={{448,0},{456,8},{464,16},{472,24},{480,32},{488,40},{496,48},{504,... | collective-permute-start | bytes 1572872 | tf_op jit(solution)/shard_map/while/body/eval_jaxpr/ppermute | solution.py:10
  403.5 27.9 %collective-permute-start = (f32[512,256]{1,0:T(8,128)S(1)}, f32[512,256]{1,0:T(8,128)S(1)}, u32[]{:S(2)}, u32[]{:S(2)}) collective-permute-start(f32[512,256]{1,0:T(8,128)S(1)} %bitcast_add_fusion.5), channel_id=1, source_target_pairs={{448,0},{456,8},{464,16},{472,24},{480,32},{488,40},{496,48},{504,... | collective-permute-start | bytes 1572872 | tf_op jit(solution)/shard_map/while/body/eval_jaxpr/ppermute | solution.py:10
  435.9 28.0 %collective-permute-start = (f32[512,256]{1,0:T(8,128)S(1)}, f32[512,256]{1,0:T(8,128)S(1)}, u32[]{:S(2)}, u32[]{:S(2)}) collective-permute-start(f32[512,256]{1,0:T(8,128)S(1)} %bitcast_add_fusion.5), channel_id=1, source_target_pairs={{448,0},{456,8},{464,16},{472,24},{480,32},{488,40},{496,48},{504,... | collective-permute-start | bytes 1572872 | tf_op jit(solution)/shard_map/while/body/eval_jaxpr/ppermute | solution.py:10
  468.3 22.1 %collective-permute-start = (f32[512,256]{1,0:T(8,128)S(1)}, f32[512,256]{1,0:T(8,128)S(1)}, u32[]{:S(2)}, u32[]{:S(2)}) collective-permute-start(f32[512,256]{1,0:T(8,128)S(1)} %bitcast_add_fusion.5), channel_id=1, source_target_pairs={{448,0},{456,8},{464,16},{472,24},{480,32},{488,40},{496,48},{504,... | collective-permute-start | bytes 1572872 | tf_op jit(solution)/shard_map/while/body/eval_jaxpr/ppermute | solution.py:10
  494.9 27.0 %collective-permute-start = (f32[512,256]{1,0:T(8,128)S(1)}, f32[512,256]{1,0:T(8,128)S(1)}, u32[]{:S(2)}, u32[]{:S(2)}) collective-permute-start(f32[512,256]{1,0:T(8,128)S(1)} %bitcast_add_fusion.5), channel_id=1, source_target_pairs={{448,0},{456,8},{464,16},{472,24},{480,32},{488,40},{496,48},{504,... | collective-permute-start | bytes 1572872 | tf_op jit(solution)/shard_map/while/body/eval_jaxpr/ppermute | solution.py:10
  521.8 28.7 %collective-permute-start.5 = (f32[512,256]{1,0:T(8,128)S(1)}, f32[512,256]{1,0:T(8,128)S(1)}, u32[]{:S(2)}, u32[]{:S(2)}) collective-permute-start(f32[512,256]{1,0:T(8,128)S(1)} %get-tuple-element.320), channel_id=1, source_target_pairs={{8,0},{16,8},{24,16},{32,24},{40,32},{48,40},{56,48},{64,56},{72,6... | collective-permute-start | bytes 1572872 | tf_op jit(solution)/shard_map/ppermute | solution.py:10
  550.6 173.8 %copy-start.1 = (bf16[128,256]{1,0:T(8,128)(2,1)S(1)}, bf16[128,256]{1,0:T(8,128)(2,1)}, u32[]{:S(2)}) copy-start(bf16[128,256]{1,0:T(8,128)(2,1)} %param.11) | copy-start | bytes 196612
  550.6 88.7 %collective-permute-start.6 = (f32[512,256]{1,0:T(8,128)S(1)}, f32[512,256]{1,0:T(8,128)S(1)}, u32[]{:S(2)}, u32[]{:S(2)}) collective-permute-start(f32[512,256]{1,0:T(8,128)S(1)} %broadcast_select_fusion), channel_id=1, source_target_pairs={{16,0},{24,8},{32,16},{40,24},{48,32},{56,40},{64,48},{72,56},{80,... | collective-permute-start | bytes 1572872 | tf_op jit(solution)/shard_map/ppermute | solution.py:10
  639.3 22.9 %collective-permute-start.7 = (f32[512,256]{1,0:T(8,128)S(1)}, f32[512,256]{1,0:T(8,128)S(1)}, u32[]{:S(2)}, u32[]{:S(2)}) collective-permute-start(f32[512,256]{1,0:T(8,128)S(1)} %broadcast_select_fusion.2), channel_id=1, source_target_pairs={{32,0},{40,8},{48,16},{56,24},{64,32},{72,40},{80,48},{88,56},{96,... | collective-permute-start | bytes 1572872 | tf_op jit(solution)/shard_map/ppermute | solution.py:10
  663.2 334.4 %all-reduce.2.cloned.1.call-start = ((), (), s32[]{:S(2)}) async-start(), calls=%async_computation.4 | async-start | bytes 262144 | tf_op jit(solution)/shard_map/psum | solution.py:124
Sparse Core Ops, SparseCore 0:
  198.4 52.2 reduce-scatter.2
  663.3 59.3 reduce-scatter.4
  728.2 269.2 all-reduce.1
where the time goes:
time: 1010 us
  waiting for transfers between devices  791 us (78%)
  starting transfers between devices  93 us (9%)
  matrix products  42.5 us (4%)
  local copies, waits for them, and re-layouts  26.1 us (3%)
  blocking collectives  22 us (2%)
  other arithmetic  16.6 us (2%)
  between operations  14 us (1%)
    ppermute x21, waiting for transfers between devices, passed_along(): return lax.ppermute(block, axis, route)  407 us
    psum x1, waiting for transfers between devices, local(): weight_grad = lax.psum(partial_grad, ('blk', 'rep'))  272 us
    ppermute x21, starting transfers between devices, passed_along(): return lax.ppermute(block, axis, route)  92.9 us
    reduce_scatter x1, waiting for transfers between devices, local(): lax.psum_scatter(carried, 'rep', scatter_dimension=0, tiled=True)  59.4 us
    reduce_scatter x1, waiting for transfers between devices, local(): pre = lax.psum_scatter(total, 'rep', scatter_dimension=0, tiled=True)  52.4 us
    all_gather x1, blocking collectives, local(): grad_rows = lax.all_gather(pre_grad, 'rep', axis=0, tiled=True)  22 us
  transfers between devices with their start and end apart: 24, of which 24 were waited for; matrix products, arithmetic and copies ran while one was open for 3% of the time, Pallas kernels for 0%

commit v1 on v0

--- a/solution.py
+++ b/solution.py
@@ -2,6 +2,11 @@
 import jax.numpy as jnp
 from jax import lax
 from jax.sharding import PartitionSpec as P
+
+
+def advance_the_modes(x_part):
+    right_arr = jax.lax.all_gather(x_part, ("blk", "rep"))
+    return jnp.sum(right_arr, 0)
 
 
 def passed_along(block, axis, distance):
@@ -121,7 +126,7 @@
     partial_grad = lax.dot_general(
         feat_rows, hidden_grad, (((0,), (0,)), ((), ())), preferred_element_type=jnp.float32
     )
-    weight_grad = lax.psum(partial_grad, ("blk", "rep"))
+    weight_grad = advance_the_modes(partial_grad)
     return (activations, feat_grad, weight_grad)
 
 

time: 1010 us -> 2260 us (2.24)
  waiting for transfers between devices: 791 us -> 2030 us
    all_gather x0 -> x1, waiting for transfers between devices: none -> 1500 us  [advance_the_modes(): right_arr = jax.lax.all_gather(x_part, ('blk', 'rep'))]
    psum x1 -> x0, waiting for transfers between devices: 272 us -> none  [local(): weight_grad = lax.psum(partial_grad, ('blk', 'rep'))]
  transfers between devices with their start and end apart: 24 -> 24, of which waited for: 24 -> 24; matrix products, arithmetic and copies ran while one was open for 3% -> 2% of each run, Pallas kernels for 0% -> 0%
where the time goes in v1:
time: 2260 us
  waiting for transfers between devices  2030 us (90%)
  starting transfers between devices  88.2 us (4%)
  matrix products  42.5 us (2%)
  other arithmetic  38.4 us (2%)
  local copies, waits for them, and re-layouts  24.5 us (1%)
    all_gather x1, waiting for transfers between devices, advance_the_modes(): right_arr = jax.lax.all_gather(x_part, ('blk', 'rep'))  1500 us
    ppermute x21, waiting for transfers between devices, passed_along(): return lax.ppermute(block, axis, route)  400 us
    ppermute x21, starting transfers between devices, passed_along(): return lax.ppermute(block, axis, route)  88.1 us
    reduce_scatter x1, waiting for transfers between devices, local(): lax.psum_scatter(carried, 'rep', scatter_dimension=0, tiled=True)  71.2 us
    reduce_scatter x1, waiting for transfers between devices, local(): pre = lax.psum_scatter(total, 'rep', scatter_dimension=0, tiled=True)  52.3 us
  transfers between devices with their start and end apart: 24, of which 24 were waited for; matrix products, arithmetic and copies ran while one was open for 2% of the time, Pallas kernels for 0%

profile of v1, /device:TPU:1, one launch (start us, length us, event | category | flops | bytes accessed | tf_op | source)
XLA Modules:
  0.0 2258.3 jit_solution(6768286756895917484)
XLA Ops:
  9.1 4.6 collective-permute-start.2
  15.0 3.9 collective-permute-done.2
  18.9 1.9 collective-permute-start.3
  21.6 14.1 collective-permute-done.3
  35.7 1.9 collective-permute-start.4
  38.4 12.9 collective-permute-done.4
  51.4 140.1 %while.34 = (s32[]{:T(128)}, bf16[512,256]{1,0:T(8,128)(2,1)S(1)}, f32[512,256]{1,0:T(8,128)S(1)}, s32[8,12]{1,0:T(8,128)S(1)}, bf16[8,12,128,128]{3,2,1,0:T(8,1...) while((s32[]{:T(128)}, bf16[512,256]{1,0:T(8,128)(2,1)S(1)}, f32[512,256]{1,0:T(8,128)S(1)}, ...), condition=%wide.region_1.2_spmd.clone, body=%wide.region_0.1_spmd.clone.sunk | while | flops 104465824 | bytes 10621531 | solution.py:97
  51.4 1.9 collective-permute-start.1
  57.8 10.0 collective-permute-done.1
  67.8 1.9 collective-permute-start.1
  74.2 13.7 collective-permute-done.1
  87.9 1.9 collective-permute-start.1
  94.3 14.5 collective-permute-done.1
  108.8 1.9 collective-permute-start.1
  115.2 14.4 collective-permute-done.1
  129.6 1.9 collective-permute-start.1
  136.0 14.3 collective-permute-done.1
  150.3 2.6 collective-permute-start.1
  157.4 12.5 collective-permute-done.1
  169.9 3.7 collective-permute-start.1
  178.1 13.4 collective-permute-done.1
  192.1 2.6 fusion.26
  194.7 2.2 copy.14
  198.3 52.3 %reduce-scatter.3.cloned.1.call-done = f32[64,256]{1,0:T(8,128)} async-done(((f32[512,256]{1,0:T(8,128)}), f32[64,256]{1,0:T(8,128)}) %reduce-scatter.3.cloned.1.call-update) | async-done | bytes 65552 | tf_op jit(solution)/shard_map/reduce_scatter | solution.py:99
  252.1 22.0 all_gather.9
  274.2 241.4 %while.33 = (s32[]{:T(128)}, f32[512,256]{1,0:T(8,128)S(1)}, s32[8,12]{1,0:T(8,128)S(1)}, bf16[8,12,128,128]{3,2,1,0:T(8,128)(2,1)}, bf16[512,256]{1,0:T(8,128)(2,1)S(1)}, /*index=5*/s32[8]{0:T(128)S(1)}, s32[]{:T(128)}) while((s32[]{:T(128)}, f32[512,256]{1,0:T(8,128)S(1)}, s32[8,12]{1,0:T(8,128)S(1)}, bf16[8,12,128,128]{3,2,1,0:T(8,128)(2,1)}, ...), condition=%wide.region_4.5_spmd, body=%wide.region_3.4_spmd.sunk | while | flops 104334752 | bytes 11146301 | solution.py:117
  278.7 6.7 collective-permute-start
  285.4 15.3 collective-permute-done
  305.2 1.9 collective-permute-start
  307.2 22.8 %collective-permute-done = f32[512,256]{1,0:T(8,128)S(1)} collective-permute-done((f32[512,256]{1,0:T(8,128)S(1)}, f32[512,256]{1,0:T(8,128)S(1)}, u32[]{:S(2)}, u32[]{:S(2)}) %collective-permute-start) | collective-permute-done | bytes 524320 | tf_op jit(solution)/shard_map/while/body/eval_jaxpr/ppermute | solution.py:15
  334.4 1.9 collective-permute-start
  336.3 28.2 %collective-permute-done = f32[512,256]{1,0:T(8,128)S(1)} collective-permute-done((f32[512,256]{1,0:T(8,128)S(1)}, f32[512,256]{1,0:T(8,128)S(1)}, u32[]{:S(2)}, u32[]{:S(2)}) %collective-permute-start) | collective-permute-done | bytes 524320 | tf_op jit(solution)/shard_map/while/body/eval_jaxpr/ppermute | solution.py:15
  369.0 1.9 collective-permute-start
  370.9 26.1 %collective-permute-done = f32[512,256]{1,0:T(8,128)S(1)} collective-permute-done((f32[512,256]{1,0:T(8,128)S(1)}, f32[512,256]{1,0:T(8,128)S(1)}, u32[]{:S(2)}, u32[]{:S(2)}) %collective-permute-start) | collective-permute-done | bytes 524320 | tf_op jit(solution)/shard_map/while/body/eval_jaxpr/ppermute | solution.py:15
  403.4 21.2 collective-permute-done
  429.1 1.9 collective-permute-start
  431.0 27.8 %collective-permute-done = f32[512,256]{1,0:T(8,128)S(1)} collective-permute-done((f32[512,256]{1,0:T(8,128)S(1)}, f32[512,256]{1,0:T(8,128)S(1)}, u32[]{:S(2)}, u32[]{:S(2)}) %collective-permute-start) | collective-permute-done | bytes 524320 | tf_op jit(solution)/shard_map/while/body/eval_jaxpr/ppermute | solution.py:15
  463.3 1.9 collective-permute-start
  465.2 24.1 %collective-permute-done = f32[512,256]{1,0:T(8,128)S(1)} collective-permute-done((f32[512,256]{1,0:T(8,128)S(1)}, f32[512,256]{1,0:T(8,128)S(1)}, u32[]{:S(2)}, u32[]{:S(2)}) %collective-permute-start) | collective-permute-done | bytes 524320 | tf_op jit(solution)/shard_map/while/body/eval_jaxpr/ppermute | solution.py:15
  495.7 19.9 collective-permute-done
  515.6 26.1 %collective-permute-start.5 = (f32[512,256]{1,0:T(8,128)S(1)}, f32[512,256]{1,0:T(8,128)S(1)}, u32[]{:S(2)}, u32[]{:S(2)}) collective-permute-start(f32[512,256]{1,0:T(8,128)S(1)} %get-tuple-element.320), channel_id=1, source_target_pairs={{8,0},{16,8},{24,16},{32,24},{40,32},{48,40},{56,48},{64,56},{72,6... | collective-permute-start | bytes 1572872 | tf_op jit(solution)/shard_map/ppermute | solution.py:15
  543.3 12.9 collective-permute-start.6
  556.2 72.5 %collective-permute-done.6 = f32[512,256]{1,0:T(8,128)S(1)} collective-permute-done((f32[512,256]{1,0:T(8,128)S(1)}, f32[512,256]{1,0:T(8,128)S(1)}, u32[]{:S(2)}, u32[]{:S(2)}) %collective-permute-start.6) | collective-permute-done | bytes 524320 | tf_op jit(solution)/shard_map/ppermute | solution.py:15
  628.8 4.6 collective-permute-start.7
  633.5 17.1 collective-permute-done.7
  651.4 71.2 %reduce-scatter.5.cloned.1.call-done = f32[64,256]{1,0:T(8,128)} async-done(((f32[512,256]{1,0:T(8,128)}), f32[64,256]{1,0:T(8,128)}) %reduce-scatter.5.cloned.1.call-update) | async-done | bytes 65552 | tf_op jit(solution)/shard_map/reduce_scatter | solution.py:119
  725.9 1504.0 %all-gather.3.cloned.1.call-done = f32[65536,256]{1,0:T(8,128)} async-done(((f32[128,256]{1,0:T(8,128)}), f32[65536,256]{1,0:T(8,128)}) %all-gather.3.cloned.1.call-update) | async-done | bytes 67108880 | tf_op jit(solution)/shard_map/all_gather | solution.py:8
  2229.9 21.8 reduce_sum.9
  (197 shorter events, 84.2 us)
Async XLA Ops:
  7.2 0.9 copy-start
  7.2 44.2 %copy-start.4 = (s32[1,1,8]{2,1,0:T(1,128)S(1)}, s32[1,1,8]{2,1,0:T(1,128)}, u32[]{:S(2)}) copy-start(s32[1,1,8]{2,1,0:T(1,128)} %param.14) | copy-start | bytes 100
  7.2 31.2 %copy-start.3 = (s32[1,1,8,12]{3,2,1,0:T(8,128)S(1)}, s32[1,1,8,12]{3,2,1,0:T(8,128)}, u32[]{:S(2)}) copy-start(s32[1,1,8,12]{3,2,1,0:T(8,128)} %param.13) | copy-start | bytes 1156
  7.2 243.4 %reduce-scatter.3.cloned.1.call-start = ((), (), s32[]{:S(2)}) async-start(), calls=%async_computation.2 | async-start | bytes 589824 | tf_op jit(solution)/shard_map/reduce_scatter | solution.py:99
  9.1 9.8 collective-permute-start.2
  18.9 16.8 collective-permute-start.3
  35.7 15.6 collective-permute-start.4
  51.4 16.4 collective-permute-start.1
  67.8 20.1 collective-permute-start.1
  87.9 20.9 collective-permute-start.1
  108.8 20.8 collective-permute-start.1
  129.6 20.7 collective-permute-start.1
  150.3 19.6 collective-permute-start.1
  169.9 21.5 collective-permute-start.1
  197.2 53.4 %copy-start.2 = (bf16[64,256]{1,0:T(8,128)(2,1)S(1)}, bf16[64,256]{1,0:T(8,128)(2,1)}, u32[]{:S(2)}) copy-start(bf16[64,256]{1,0:T(8,128)(2,1)} %param.15) | copy-start | bytes 98308
  198.3 524.3 %reduce-scatter.5.cloned.1.call-start = ((), (), s32[]{:S(2)}) async-start(), calls=%async_computation.3 | async-start | bytes 589824 | tf_op jit(solution)/shard_map/reduce_scatter | solution.py:119
  278.7 22.1 collective-permute-start
  305.2 24.7 %collective-permute-start = (f32[512,256]{1,0:T(8,128)S(1)}, f32[512,256]{1,0:T(8,128)S(1)}, u32[]{:S(2)}, u32[]{:S(2)}) collective-permute-start(f32[512,256]{1,0:T(8,128)S(1)} %bitcast_add_fusion.5), channel_id=1, source_target_pairs={{448,0},{456,8},{464,16},{472,24},{480,32},{488,40},{496,48},{504,... | collective-permute-start | bytes 1572872 | tf_op jit(solution)/shard_map/while/body/eval_jaxpr/ppermute | solution.py:15
  334.4 30.1 %collective-permute-start = (f32[512,256]{1,0:T(8,128)S(1)}, f32[512,256]{1,0:T(8,128)S(1)}, u32[]{:S(2)}, u32[]{:S(2)}) collective-permute-start(f32[512,256]{1,0:T(8,128)S(1)} %bitcast_add_fusion.5), channel_id=1, source_target_pairs={{448,0},{456,8},{464,16},{472,24},{480,32},{488,40},{496,48},{504,... | collective-permute-start | bytes 1572872 | tf_op jit(solution)/shard_map/while/body/eval_jaxpr/ppermute | solution.py:15
  369.0 28.0 %collective-permute-start = (f32[512,256]{1,0:T(8,128)S(1)}, f32[512,256]{1,0:T(8,128)S(1)}, u32[]{:S(2)}, u32[]{:S(2)}) collective-permute-start(f32[512,256]{1,0:T(8,128)S(1)} %bitcast_add_fusion.5), channel_id=1, source_target_pairs={{448,0},{456,8},{464,16},{472,24},{480,32},{488,40},{496,48},{504,... | collective-permute-start | bytes 1572872 | tf_op jit(solution)/shard_map/while/body/eval_jaxpr/ppermute | solution.py:15
  401.5 23.1 %collective-permute-start = (f32[512,256]{1,0:T(8,128)S(1)}, f32[512,256]{1,0:T(8,128)S(1)}, u32[]{:S(2)}, u32[]{:S(2)}) collective-permute-start(f32[512,256]{1,0:T(8,128)S(1)} %bitcast_add_fusion.5), channel_id=1, source_target_pairs={{448,0},{456,8},{464,16},{472,24},{480,32},{488,40},{496,48},{504,... | collective-permute-start | bytes 1572872 | tf_op jit(solution)/shard_map/while/body/eval_jaxpr/ppermute | solution.py:15
  429.1 29.7 %collective-permute-start = (f32[512,256]{1,0:T(8,128)S(1)}, f32[512,256]{1,0:T(8,128)S(1)}, u32[]{:S(2)}, u32[]{:S(2)}) collective-permute-start(f32[512,256]{1,0:T(8,128)S(1)} %bitcast_add_fusion.5), channel_id=1, source_target_pairs={{448,0},{456,8},{464,16},{472,24},{480,32},{488,40},{496,48},{504,... | collective-permute-start | bytes 1572872 | tf_op jit(solution)/shard_map/while/body/eval_jaxpr/ppermute | solution.py:15
  463.3 26.0 %collective-permute-start = (f32[512,256]{1,0:T(8,128)S(1)}, f32[512,256]{1,0:T(8,128)S(1)}, u32[]{:S(2)}, u32[]{:S(2)}) collective-permute-start(f32[512,256]{1,0:T(8,128)S(1)} %bitcast_add_fusion.5), channel_id=1, source_target_pairs={{448,0},{456,8},{464,16},{472,24},{480,32},{488,40},{496,48},{504,... | collective-permute-start | bytes 1572872 | tf_op jit(solution)/shard_map/while/body/eval_jaxpr/ppermute | solution.py:15
  493.8 21.8 collective-permute-start
  515.6 27.6 %collective-permute-start.5 = (f32[512,256]{1,0:T(8,128)S(1)}, f32[512,256]{1,0:T(8,128)S(1)}, u32[]{:S(2)}, u32[]{:S(2)}) collective-permute-start(f32[512,256]{1,0:T(8,128)S(1)} %get-tuple-element.320), channel_id=1, source_target_pairs={{8,0},{16,8},{24,16},{32,24},{40,32},{48,40},{56,48},{64,56},{72,6... | collective-permute-start | bytes 1572872 | tf_op jit(solution)/shard_map/ppermute | solution.py:15
  543.3 181.1 %copy-start.1 = (bf16[128,256]{1,0:T(8,128)(2,1)S(1)}, bf16[128,256]{1,0:T(8,128)(2,1)}, u32[]{:S(2)}) copy-start(bf16[128,256]{1,0:T(8,128)(2,1)} %param.11) | copy-start | bytes 196612
  543.3 85.5 %collective-permute-start.6 = (f32[512,256]{1,0:T(8,128)S(1)}, f32[512,256]{1,0:T(8,128)S(1)}, u32[]{:S(2)}, u32[]{:S(2)}) collective-permute-start(f32[512,256]{1,0:T(8,128)S(1)} %broadcast_select_fusion), channel_id=1, source_target_pairs={{16,0},{24,8},{32,16},{40,24},{48,32},{56,40},{64,48},{72,56},{80,... | collective-permute-start | bytes 1572872 | tf_op jit(solution)/shard_map/ppermute | solution.py:15
  628.8 21.7 collective-permute-start.7
  651.4 1578.5 %all-gather.3.cloned.1.call-start = ((), (), s32[]{:S(2)}) async-start(), calls=%async_computation.4 | async-start | bytes 67239936 | tf_op jit(solution)/shard_map/all_gather | solution.py:8
Sparse Core Ops, SparseCore 0:
  198.4 52.2 reduce-scatter.2
  651.5 71.0 reduce-scatter.4
  725.4 1504.4 all-gather.2
